TPU v7x, 32 devices: a whole 2x2x4 slice. The times are simulated.
32 devices in a mesh: tm: 16 (over z, y, x), tensor: 2 (over core).
Axes of the slice: x: 2, y: 2, z: 4, core: 2. Of those that a mesh axis runs over, the one named last changes fastest.
Arguments:
- frames: bfloat16 [32768, 1024], P('tm'), may hold values from -6 to 6
- utt_ids: int32 [32768], P('tm'), may hold values from 0 to 63, never falling along the last dimension, each value on 1 to 1024 neighbouring positions
- seg_ids: int32 [32768], P('tm'), may hold values from 0 to 1023, as said below
- norm_gain: float32 [1024], replicated, may hold values from 0.1 to 1.9
- w_value: bfloat16 [1024, 1024], P(None, 'tensor'), may hold values from -0.1875 to 0.1875
- w_gate: bfloat16 [1024, 1024], P(None, 'tensor'), may hold values from -0.1875 to 0.1875
- conv_taps: float32 [31, 1024], P(None, 'tensor'), may hold values from -2 to 2
- bn_scale: float32 [1024], P('tensor'), may hold values from 0.1 to 1.9
- bn_shift: float32 [1024], P('tensor'), may hold values from -3 to 3
- w_out: bfloat16 [1024, 1024], P('tensor'), may hold values from -0.375 to 0.375
Outputs:
- compressed: float32 [1024, 1024], P('tm', 'tensor')
Inputs may be any that keep to these rules, and one draw needn't show every extreme that they name: `seg_ids`: never falling; segment s is owned by index s // 64 of tm, each owner has 64 segments of one or more frames; the frames of index i of tm name only segments owned by indices i and i + 1, the latter only in its last 256 frames. `utt_ids`: never falling; each utterance has 1 to 1024 frames.
All inputs are finite; a program needn't handle non-finite values.
Results may differ from a plain program's by a relative error of at most 0.008.
Values may be sent and summed in bfloat16 or wider, within the bound.
A program may use at most 64 MiB of HBM per device.

v0:
```python
import jax
import jax.numpy as jnp
from jax import lax
from jax.sharding import PartitionSpec as P


def padded_2(block, sides, width):
    for axis, dim in sides:
        count = lax.axis_size(axis)
        forward = [(i, i + 1) for i in range(count - 1)]
        backward = [(target, source) for source, target in forward]
        low = lax.ppermute(
            lax.slice_in_dim(block, block.shape[dim] - width, None, axis=dim), axis, forward
        )
        high = lax.ppermute(lax.slice_in_dim(block, 0, width, axis=dim), axis, backward)
        block = jnp.concatenate([low, block, high], axis=dim)
    return block


def from_behind(value, axis, steps):
    count = lax.axis_size(axis)
    leading, last = (max(0, -steps), min(count, count - steps))
    return lax.ppermute(value, axis, [(source, source + steps) for source in range(leading, last)])


def shards(
    frames, utt_ids, seg_ids, norm_gain, w_value, w_gate, conv_taps, bn_scale, bn_shift, w_out
):
    rows = frames.shape[0]
    channels = w_value.shape[1]
    owned = rows // 32
    floats = frames.astype(jnp.float32)
    center = jnp.mean(floats, axis=1, keepdims=True)
    spread = jnp.mean((floats - center) ** 2, axis=1, keepdims=True)
    normed = ((floats - center) * lax.rsqrt(spread + 1e-05) * norm_gain).astype(jnp.bfloat16)
    value = jnp.dot(normed, w_value, preferred_element_type=jnp.float32)
    gate = jnp.dot(normed, w_gate, preferred_element_type=jnp.float32)
    glu = (value * jax.nn.sigmoid(gate)).astype(jnp.bfloat16)
    labels = (utt_ids % 64).astype(jnp.bfloat16)
    kernel = conv_taps.shape[0]
    half = (kernel - 1) // 2
    padded, padded_labels = (
        padded_2(glu, (("tm", 0),), half),
        padded_2(labels, (("tm", 0),), half),
    )
    edge_low = lax.axis_index("tm") == 0
    edge_high = lax.axis_index("tm") == lax.axis_size("tm") - 1
    position = jnp.arange(rows + 2 * half)
    exists = jnp.where((position < half) & edge_low, 0.0, 1.0) * jnp.where(
        (position >= rows + half) & edge_high, 0.0, 1.0
    )
    conv = jnp.zeros((rows, channels), jnp.float32)
    for tap in range(kernel):
        same = (padded_labels[tap : tap + rows] == labels).astype(jnp.float32) * exists[
            tap : tap + rows
        ]
        conv = conv + conv_taps[tap] * (
            padded[tap : tap + rows].astype(jnp.float32) * same[:, None]
        )
    hidden = jax.nn.silu(conv * bn_scale + bn_shift).astype(jnp.bfloat16)
    column = lax.axis_index("tensor") * channels
    frame_cols = lax.dynamic_slice_in_dim(frames, column, channels, 1)
    index = lax.axis_index("tm")
    slots = seg_ids - index * owned
    onehot = (jnp.arange(2 * owned, dtype=jnp.int32)[:, None] == slots[None, :]).astype(
        jnp.bfloat16
    )
    pooled = jnp.concatenate(
        [
            jnp.dot(onehot, hidden, preferred_element_type=jnp.float32),
            jnp.dot(onehot, frame_cols, preferred_element_type=jnp.float32),
        ],
        axis=1,
    )
    tallies = jnp.sum(onehot.astype(jnp.float32), axis=1)
    blocks = pooled.reshape(2, owned, 2 * channels)
    tally_blocks = tallies.reshape(2, owned)
    left_sum, left_tally = (
        from_behind(blocks[1].astype(jnp.bfloat16), "tm", 1).astype(jnp.float32),
        from_behind(tally_blocks[1].astype(jnp.bfloat16), "tm", 1).astype(jnp.float32),
    )
    totals = blocks[0] + left_sum
    count = tally_blocks[0] + left_tally
    means = totals / count[:, None]
    mean_hidden = means[:, :channels].astype(jnp.bfloat16)
    mean_frames = means[:, channels:]
    partial_value = jnp.dot(mean_hidden, w_out, preferred_element_type=jnp.float32)
    mixed = lax.psum_scatter(
        partial_value.astype(jnp.bfloat16), "tensor", scatter_dimension=1, tiled=True
    ).astype(jnp.float32)
    return mean_frames + mixed


def solution(mesh):
    in_specs = (
        P("tm", None),
        P("tm"),
        P("tm"),
        P(),
        P(None, "tensor"),
        P(None, "tensor"),
        P(None, "tensor"),
        P("tensor"),
        P("tensor"),
        P("tensor", None),
    )
    out_specs = P("tm", "tensor")
    return jax.shard_map(shards, mesh=mesh, in_specs=in_specs, out_specs=out_specs, check_vma=False)
```

profile of v0, /device:TPU:8, one launch (start us, length us, event | category | flops | bytes accessed | tf_op | source)
XLA Modules:
  0.0 96.8 jit_solution(2621028153230125487)
XLA Ops:
  6.5 3.0 %convert_reduce_fusion = f32[2048]{0:T(1024)S(1)} fusion(bf16[2048,1024]{1,0:T(8,128)(2,1)} %param.10), kind=kLoop, calls=%fused_computation.29 | loop fusion | flops 4192256 | bytes 4202496 | tf_op jit(solution)/shard_map/reduce_sum | solution.py:33
  9.5 0.6 copy-done.1
  10.1 1.4 %fusion.2 = f32[2048]{0:T(1024)S(1)} fusion(bf16[2048,1024]{1,0:T(8,128)(2,1)S(1)} %copy-done.1, f32[2048]{0:T(1024)S(1)} %broadcast_multiply_fusion), kind=kLoop, calls=%fused_computation.32 | loop fusion | flops 8386560 | bytes 4210688 | tf_op jit(solution)/shard_map/reduce_sum | solution.py:34
  11.5 0.0 copy-start.6
  11.5 2.7 %fusion.79 = f32[2048,512]{1,0:T(8,128)S(1)} fusion(bf16[1024,512]{1,0:T(8,128)(2,1)S(1)} %copy-done, bf16[2048,1024]{1,0:T(8,128)(2,1)S(1)} %copy-done.1, f32[1024]{0:T(1024)S(1)} %copy-done.7, f32[2048]{0:T(1024)S(1)} %add_rsqrt_fusion, f32[2048]{0:T(1024)S(1)} %broadcast_multiply_fusion), kind=kOutput, calls=%fused_computation.235 | convolution fusion | flops 2157969408 | bytes 9457664 | tf_op jit(solution)/shard_map/dot_general | solution.py:36
  14.2 0.0 copy-start.4
  14.3 0.0 copy-start.3
  14.3 0.0 copy-start.8
  14.3 4.1 %multiply_convert_fusion.1 = bf16[2048,512]{1,0:T(8,128)(2,1)S(1)} fusion(f32[2048,512]{1,0:T(8,128)S(1)} %fusion.79, bf16[1024,512]{1,0:T(8,128)(2,1)S(1)} %copy-done.6, bf16[2048,1024]{1,0:T(8,128)(2,1)S(1)} %copy-done.1, f32[1024]{0:T(1024)S(1)} %copy-done.7, f32[2048]{0:T(1024)S(1)} %add_rsqrt_fusion, f32[2048]{0:T(1024)S(1)} %broadcast_multiply_fusion), kind=kOutput, calls=%fused_computation.36 | convolution fusion | flops 2163212288 | bytes 11554816 | tf_op jit(solution)/shard_map/dot_general | solution.py:37
  18.4 4.2 %collective-permute-start.2 = (bf16[15,512]{1,0:T(8,128)(2,1)S(1)}, bf16[15,512]{1,0:T(8,128)(2,1)S(1)}, u32[]{:S(2)}, u32[]{:S(2)}) collective-permute-start(bf16[15,512]{1,0:T(8,128)(2,1)S(1)} %get-tuple-element.8), channel_id=1, source_target_pairs={{2,0},{4,2},{6,4},{8,6},{10,8},{12,10},{14,12},{16,14},{18,16},{20... | collective-permute-start | bytes 46088 | tf_op jit(solution)/shard_map/ppermute | solution.py:15
  22.6 1.9 %collective-permute-start = (bf16[15,512]{1,0:T(8,128)(2,1)S(1)}, bf16[15,512]{1,0:T(8,128)(2,1)S(1)}, u32[]{:S(2)}, u32[]{:S(2)}) collective-permute-start(bf16[15,512]{1,0:T(8,128)(2,1)S(1)} %get-tuple-element.7), channel_id=1, source_target_pairs={{0,2},{2,4},{4,6},{6,8},{8,10},{10,12},{12,14},{14,16},{16,18},{18... | collective-permute-start | bytes 46088 | tf_op jit(solution)/shard_map/ppermute | solution.py:12
  24.6 0.1 slice_select_fusion.15
  24.7 0.1 fusion.85
  24.7 5.7 %collective-permute-start.3 = (bf16[15]{0:T(256)(128)(2,1)S(1)}, bf16[15]{0:T(256)(128)(2,1)S(1)}, u32[]{:S(2)}, u32[]{:S(2)}) collective-permute-start(bf16[15]{0:T(256)(128)(2,1)S(1)} %get-tuple-element.74), channel_id=1, source_target_pairs={{2,0},{4,2},{6,4},{8,6},{10,8},{12,10},{14,12},{16,14},{18,16},{20... | collective-permute-start | bytes 98 | tf_op jit(solution)/shard_map/ppermute | solution.py:15
  30.4 1.9 %collective-permute-start.1 = (bf16[15]{0:T(256)(128)(2,1)S(1)}, bf16[15]{0:T(256)(128)(2,1)S(1)}, u32[]{:S(2)}, u32[]{:S(2)}) collective-permute-start(bf16[15]{0:T(256)(128)(2,1)S(1)} %get-tuple-element.73), channel_id=1, source_target_pairs={{0,2},{2,4},{4,6},{6,8},{8,10},{10,12},{12,14},{14,16},{16,18},{18... | collective-permute-start | bytes 98 | tf_op jit(solution)/shard_map/ppermute | solution.py:12
  32.4 0.2 convert_reduce_fusion.1
  32.6 0.1 slice.592
  32.7 3.3 %collective-permute-start.5 = (bf16[64]{0:T(256)(128)(2,1)S(1)}, bf16[64]{0:T(256)(128)(2,1)S(1)}, u32[]{:S(2)}, u32[]{:S(2)}) collective-permute-start(bf16[64]{0:T(256)(128)(2,1)S(1)} %slice.592), channel_id=1, source_target_pairs={{0,2},{2,4},{4,6},{6,8},{8,10},{10,12},{12,14},{14,16},{16,18},{18... | collective-permute-start | bytes 392 | tf_op jit(solution)/shard_map/ppermute | solution.py:23
  36.0 2.0 %fusion.33 = f32[128,512]{1,0:T(8,128)S(1)} fusion(bf16[2048,1024]{1,0:T(8,128)(2,1)} %param.10, s32[]{:T(128)S(6)} %select_n.20, s32[2048]{0:T(1024)S(1)} %broadcast_subtract_fusion), kind=kOutput, calls=%fused_computation.83 | convolution fusion | flops 268697600 | bytes 2367492 | tf_op jit(solution)/shard_map/dot_general | solution.py:71
  38.1 0.1 slice_select_fusion.14
  38.2 0.1 slice_select_fusion.13
  38.3 0.1 slice_select_fusion.28
  38.4 0.1 slice_select_fusion.30
  38.5 0.1 slice_select_fusion.29
  38.7 32.0 %fusion.35 = f32[128,512]{1,0:T(8,128)S(1)} fusion(bf16[2048,512]{1,0:T(8,128)(2,1)S(1)} %multiply_convert_fusion.1, bf16[15,512]{1,0:T(8,128)(2,1)S(1)} %collective-permute-done.2, bf16[15,512]{1,0:T(8,128)(2,1)S(1)} %collective-permute-done, f32[512]{0:T(512)S(1)} %copy-done.8, f32[512]{0:T(512)S(1)} %copy-done.9, f32[2048]{0:T(1024)S(1)} %get-tuple-element.56, ...), kind=kOutput, calls=%fused_computation.85 | convolution fusion | flops 499384320 | bytes 2719744 | tf_op jit(solution)/shard_map/dot_general | solution.py:70
  70.6 2.9 %collective-permute-start.4 = (bf16[64,1024]{1,0:T(8,128)(2,1)S(1)}, bf16[64,1024]{1,0:T(8,128)(2,1)S(1)}, u32[]{:S(2)}, u32[]{:S(2)}) collective-permute-start(bf16[64,1024]{1,0:T(8,128)(2,1)S(1)} %fusion.42), channel_id=1, source_target_pairs={{0,2},{2,4},{4,6},{6,8},{8,10},{10,12},{12,14},{14,16},{16,18},{18... | collective-permute-start | bytes 393224 | tf_op jit(solution)/shard_map/ppermute | solution.py:23
  73.5 5.8 %collective-permute-done.4 = bf16[64,1024]{1,0:T(8,128)(2,1)S(1)} collective-permute-done((bf16[64,1024]{1,0:T(8,128)(2,1)S(1)}, bf16[64,1024]{1,0:T(8,128)(2,1)S(1)}, u32[]{:S(2)}, u32[]{:S(2)}) %collective-permute-start.4) | collective-permute-done | bytes 131104 | tf_op jit(solution)/shard_map/ppermute | solution.py:23
  79.3 0.1 fusion.41
  79.4 1.0 convolution_convert_fusion
  80.4 0.0 reduce-scatter.2.cloned.1.call-update
  80.4 8.0 %reduce-scatter.2.cloned.1.call-done = bf16[64,512]{1,0:T(8,128)(2,1)} async-done(((bf16[64,1024]{1,0:T(8,128)(2,1)}), bf16[64,512]{1,0:T(8,128)(2,1)}) %reduce-scatter.2.cloned.1.call-update) | async-done | bytes 65552 | tf_op jit(solution)/shard_map/reduce_scatter | solution.py:88
  88.4 1.5 %slice_add_fusion = f32[64,512]{1,0:T(8,128)} fusion(f32[64,1024]{1,0:T(8,128)S(1)} %fusion.41, bf16[64,512]{1,0:T(8,128)(2,1)} %reduce-scatter.2.cloned.1.call-done), kind=kLoop, calls=%fused_computation.100 | loop fusion | flops 65536 | bytes 327680 | tf_op jit(solution)/shard_map/add | solution.py:91
  (31 shorter events, 0.2 us)
Async XLA Ops:
  6.5 5.0 %copy-start = (bf16[1024,512]{1,0:T(8,128)(2,1)S(1)}, bf16[1024,512]{1,0:T(8,128)(2,1)}, u32[]{:S(2)}) copy-start(bf16[1024,512]{1,0:T(8,128)(2,1)} %param.14) | copy-start | bytes 3145732
  6.5 5.0 %copy-start.7 = (f32[1024]{0:T(1024)S(1)}, f32[1024]{0:T(1024)}, u32[]{:S(2)}) copy-start(f32[1024]{0:T(1024)} %param.13) | copy-start | bytes 12292
  6.5 81.9 %reduce-scatter.2.cloned.1.call-start = ((), (), s32[]{:S(2)}) async-start(), calls=%async_computation.1 | async-start | bytes 196608 | tf_op jit(solution)/shard_map/reduce_scatter | solution.py:88
  6.5 3.5 %copy-start.1 = (bf16[2048,1024]{1,0:T(8,128)(2,1)S(1)}, bf16[2048,1024]{1,0:T(8,128)(2,1)}, u32[]{:S(2)}) copy-start(bf16[2048,1024]{1,0:T(8,128)(2,1)} %param.10) | copy-start | bytes 12582916
  11.5 2.7 %copy-start.6 = (bf16[1024,512]{1,0:T(8,128)(2,1)S(1)}, bf16[1024,512]{1,0:T(8,128)(2,1)}, u32[]{:S(2)}) copy-start(bf16[1024,512]{1,0:T(8,128)(2,1)} %param.15) | copy-start | bytes 3145732
  14.2 10.3 %copy-start.4 = (s32[2048]{0:T(1024)S(1)}, s32[2048]{0:T(1024)}, u32[]{:S(2)}) copy-start(s32[2048]{0:T(1024)} %param.11) | copy-start | bytes 24580
  14.2 18.1 %copy-start.5 = (s32[2048]{0:T(1024)S(1)}, s32[2048]{0:T(1024)}, u32[]{:S(2)}) copy-start(s32[2048]{0:T(1024)} %param.12) | copy-start | bytes 24580
  14.3 21.7 %copy-start.3 = (f32[31,512]{1,0:T(8,128)S(1)}, f32[31,512]{1,0:T(8,128)}, u32[]{:S(2)}) copy-start(f32[31,512]{1,0:T(8,128)} %param.16) | copy-start | bytes 190468
  14.3 24.4 %copy-start.8 = (f32[512]{0:T(512)S(1)}, f32[512]{0:T(512)}, u32[]{:S(2)}) copy-start(f32[512]{0:T(512)} %param.18) | copy-start | bytes 6148
  14.3 24.4 %copy-start.9 = (f32[512]{0:T(512)S(1)}, f32[512]{0:T(512)}, u32[]{:S(2)}) copy-start(f32[512]{0:T(512)} %param.17) | copy-start | bytes 6148
  18.4 20.2 %collective-permute-start.2 = (bf16[15,512]{1,0:T(8,128)(2,1)S(1)}, bf16[15,512]{1,0:T(8,128)(2,1)S(1)}, u32[]{:S(2)}, u32[]{:S(2)}) collective-permute-start(bf16[15,512]{1,0:T(8,128)(2,1)S(1)} %get-tuple-element.8), channel_id=1, source_target_pairs={{2,0},{4,2},{6,4},{8,6},{10,8},{12,10},{14,12},{16,14},{18,16},{20... | collective-permute-start | bytes 46088 | tf_op jit(solution)/shard_map/ppermute | solution.py:15
  22.6 16.0 %collective-permute-start = (bf16[15,512]{1,0:T(8,128)(2,1)S(1)}, bf16[15,512]{1,0:T(8,128)(2,1)S(1)}, u32[]{:S(2)}, u32[]{:S(2)}) collective-permute-start(bf16[15,512]{1,0:T(8,128)(2,1)S(1)} %get-tuple-element.7), channel_id=1, source_target_pairs={{0,2},{2,4},{4,6},{6,8},{8,10},{10,12},{12,14},{14,16},{16,18},{18... | collective-permute-start | bytes 46088 | tf_op jit(solution)/shard_map/ppermute | solution.py:12
  24.7 13.3 %collective-permute-start.3 = (bf16[15]{0:T(256)(128)(2,1)S(1)}, bf16[15]{0:T(256)(128)(2,1)S(1)}, u32[]{:S(2)}, u32[]{:S(2)}) collective-permute-start(bf16[15]{0:T(256)(128)(2,1)S(1)} %get-tuple-element.74), channel_id=1, source_target_pairs={{2,0},{4,2},{6,4},{8,6},{10,8},{12,10},{14,12},{16,14},{18,16},{20... | collective-permute-start | bytes 98 | tf_op jit(solution)/shard_map/ppermute | solution.py:15
  30.4 7.8 %collective-permute-start.1 = (bf16[15]{0:T(256)(128)(2,1)S(1)}, bf16[15]{0:T(256)(128)(2,1)S(1)}, u32[]{:S(2)}, u32[]{:S(2)}) collective-permute-start(bf16[15]{0:T(256)(128)(2,1)S(1)} %get-tuple-element.73), channel_id=1, source_target_pairs={{0,2},{2,4},{4,6},{6,8},{8,10},{10,12},{12,14},{14,16},{16,18},{18... | collective-permute-start | bytes 98 | tf_op jit(solution)/shard_map/ppermute | solution.py:12
  32.7 40.8 %collective-permute-start.5 = (bf16[64]{0:T(256)(128)(2,1)S(1)}, bf16[64]{0:T(256)(128)(2,1)S(1)}, u32[]{:S(2)}, u32[]{:S(2)}) collective-permute-start(bf16[64]{0:T(256)(128)(2,1)S(1)} %slice.592), channel_id=1, source_target_pairs={{0,2},{2,4},{4,6},{6,8},{8,10},{10,12},{12,14},{14,16},{16,18},{18... | collective-permute-start | bytes 392 | tf_op jit(solution)/shard_map/ppermute | solution.py:23
  38.6 40.8 %copy-start.2 = (bf16[512,1024]{1,0:T(8,128)(2,1)S(1)}, bf16[512,1024]{1,0:T(8,128)(2,1)}, u32[]{:S(2)}) copy-start(bf16[512,1024]{1,0:T(8,128)(2,1)} %param.19) | copy-start | bytes 3145732
  70.6 8.7 %collective-permute-start.4 = (bf16[64,1024]{1,0:T(8,128)(2,1)S(1)}, bf16[64,1024]{1,0:T(8,128)(2,1)S(1)}, u32[]{:S(2)}, u32[]{:S(2)}) collective-permute-start(bf16[64,1024]{1,0:T(8,128)(2,1)S(1)} %fusion.42), channel_id=1, source_target_pairs={{0,2},{2,4},{4,6},{6,8},{8,10},{10,12},{12,14},{14,16},{16,18},{18... | collective-permute-start | bytes 393224 | tf_op jit(solution)/shard_map/ppermute | solution.py:23
Sparse Core Ops, SparseCore 0:
  80.5 7.8 reduce-scatter.1
where the time goes:
time: 98.4 us; the launch traced here: 96.8 us
  matrix products  41.7 us (42%)
  starting transfers between devices  19.9 us (20%)
  waiting for transfers between devices  13.8 us (14%)
  between operations  13.8 us (14%)
  other arithmetic  6.73 us (7%)
    dot_general x1, matrix products, shards(): jnp.dot(onehot, hidden, preferred_element_type=jnp.float32)  32 us
    ppermute x2, starting transfers between devices, padded_2(): lax.ppermute(lax.slice_in_dim(block, 0, width, axis=dim), axis, backward)  9.95 us
    reduce_scatter x1, waiting for transfers between devices, shards(): lax.psum_scatter(partial_value.astype(jnp.bfloat16), 'tensor', scatter_di...  8.02 us
    ppermute x2, starting transfers between devices, from_behind(): lax.ppermute(value, axis, [(source, source + steps) for source in range(l...  6.12 us
    ppermute x2, waiting for transfers between devices, from_behind(): lax.ppermute(value, axis, [(source, source + steps) for source in range(l...  5.76 us
    dot_general x1, matrix products, shards(): gate = jnp.dot(normed, w_gate, preferred_element_type=jnp.float32)  4.05 us
    ppermute x2, starting transfers between devices, padded_2(): lax.ppermute(lax.slice_in_dim(block, block.shape[dim] - width, None, axis...  3.84 us
    reduce_sum x1, other arithmetic, shards(): center = jnp.mean(floats, axis=1, keepdims=True)  2.95 us
  transfers between devices with their start and end apart: 7, of which 2 were waited for; matrix products, arithmetic and copies ran while one was open for 36% of the time, Pallas kernels for 0%

commit v1 on v0

v1 whole, which is shorter than its diff:
```python
import functools

import jax
import jax.numpy as jnp
from jax import lax
from jax.experimental import pallas as pl
from jax.experimental.pallas import tpu as pltpu
from jax.sharding import PartitionSpec as P

MESH = pl.DeviceIdType.MESH
VMEM = pl.BlockSpec(memory_space=pltpu.VMEM)
HBM = pl.BlockSpec(memory_space=pltpu.HBM)
EDGE = 16
LANES = 128
CHUNK = 256
SUB = 64
MIB = 1 << 20


def sigmoid(v):
    return 0.5 + 0.5 * jnp.tanh(0.5 * v)


def normalised(block, gain):
    floats = block.astype(jnp.float32)
    center = jnp.mean(floats, axis=1, keepdims=True)
    moved = floats - center
    spread = jnp.mean(moved * moved, axis=1, keepdims=True)
    return (moved * lax.rsqrt(spread + 1e-05) * gain).astype(jnp.bfloat16)


def selection(slots, slot_count):
    kinds = lax.broadcasted_iota(jnp.int32, (slot_count, LANES), 0)
    rows = [
        jnp.where(kinds == slots[r : r + 1, :], 1.0, 0.0).astype(jnp.bfloat16)
        for r in range(slots.shape[0])
    ]
    return jnp.concatenate(rows, axis=1)


def glu_kernel(
    tm_count, frames, labels, segs, gain, wv_hbm, wg_hbm,
    glu_out, lab_out, pooled_out,
    held, normed, halo, lab_low, lab_high, wv, wg, chunk_sems, w_sems, send, recv,
):
    rows = frames.shape[0]
    channels = wv.shape[1]
    chunks = rows // CHUNK
    lab_rows = labels.shape[0]
    owned = rows // 32
    me = lax.axis_index("tm")
    column = lax.axis_index("tensor")
    loads = [
        pltpu.make_async_copy(
            frames.at[pl.ds(k * CHUNK, CHUNK)], held.at[pl.ds(k * CHUNK, CHUNK)], chunk_sems.at[k]
        )
        for k in range(chunks)
    ]
    weights = [
        pltpu.make_async_copy(wv_hbm, wv, w_sems.at[0]),
        pltpu.make_async_copy(wg_hbm, wg, w_sems.at[1]),
    ]
    loads[0].start()
    for copy in weights + loads[1:]:
        copy.start()
    up = {"tm": me + 1}
    down = {"tm": me - 1}
    ups = [
        pltpu.make_async_remote_copy(
            frames.at[pl.ds(rows - EDGE, EDGE)], halo.at[pl.ds(0, EDGE)],
            send.at[0], recv.at[0], device_id=up, device_id_type=MESH,
        ),
        pltpu.make_async_remote_copy(
            labels.at[pl.ds(lab_rows - 8, 8)], lab_low,
            send.at[1], recv.at[1], device_id=up, device_id_type=MESH,
        ),
    ]
    downs = [
        pltpu.make_async_remote_copy(
            frames.at[pl.ds(0, EDGE)], halo.at[pl.ds(EDGE, EDGE)],
            send.at[2], recv.at[2], device_id=down, device_id_type=MESH,
        ),
        pltpu.make_async_remote_copy(
            labels.at[pl.ds(0, 8)], lab_high,
            send.at[3], recv.at[3], device_id=down, device_id_type=MESH,
        ),
    ]
    has_low = me > 0
    has_high = me < tm_count - 1
    barrier = pltpu.get_barrier_semaphore()

    @pl.when(has_low)
    def _():
        pl.semaphore_signal(barrier, inc=1, device_id=down, device_id_type=MESH)

    @pl.when(has_high)
    def _():
        pl.semaphore_signal(barrier, inc=1, device_id=up, device_id_type=MESH)

    inner = jnp.logical_and(has_low, has_high)

    @pl.when(inner)
    def _():
        pl.semaphore_wait(barrier, 2)

    @pl.when(jnp.logical_not(inner))
    def _():
        pl.semaphore_wait(barrier, 1)

    @pl.when(has_high)
    def _():
        for copy in ups:
            copy.start()

    @pl.when(has_low)
    def _():
        for copy in downs:
            copy.start()

    @pl.when(jnp.logical_not(has_low))
    def _():
        halo[pl.ds(0, EDGE), :] = jnp.zeros((EDGE, halo.shape[1]), halo.dtype)
        lab_low[...] = jnp.full(lab_low.shape, -1, jnp.int32)

    @pl.when(jnp.logical_not(has_high))
    def _():
        halo[pl.ds(EDGE, EDGE), :] = jnp.zeros((EDGE, halo.shape[1]), halo.dtype)
        lab_high[...] = jnp.full(lab_high.shape, -1, jnp.int32)

    scale = gain[...]
    columns = pl.ds(pl.multiple_of(column * channels, LANES), channels)
    per = CHUNK // LANES
    pooled = jnp.zeros((2 * owned, channels), jnp.float32)

    def prepare(k):
        loads[k].wait()
        normed[k % 2, pl.ds(0, CHUNK), :] = normalised(held[pl.ds(k * CHUNK, CHUNK), :], scale)

    prepare(0)
    for copy in weights:
        copy.wait()
    for k in range(chunks):
        if k + 1 < chunks:
            prepare(k + 1)
        size = CHUNK
        if k == chunks - 1:
            size = CHUNK + 2 * EDGE

            @pl.when(has_low)
            def _():
                ups[0].wait_recv()
                ups[1].wait_recv()

            @pl.when(has_high)
            def _():
                downs[0].wait_recv()
                downs[1].wait_recv()

            normed[k % 2, pl.ds(CHUNK, 2 * EDGE), :] = normalised(halo[...], scale)
        block = normed[k % 2, pl.ds(0, size), :]
        value = jnp.dot(block, wv[...], preferred_element_type=jnp.float32)
        gate = jnp.dot(block, wg[...], preferred_element_type=jnp.float32)
        glu = (value * sigmoid(gate)).astype(jnp.bfloat16)
        glu_out[pl.ds(EDGE + k * CHUNK, CHUNK), :] = glu[:CHUNK]
        if k == chunks - 1:
            glu_out[pl.ds(0, EDGE), :] = glu[CHUNK : CHUNK + EDGE]
            glu_out[pl.ds(EDGE + rows, EDGE), :] = glu[CHUNK + EDGE :]
        slots = segs[pl.ds(k * per, per), :] - me * owned
        pooled = pooled + jnp.dot(
            selection(slots, 2 * owned),
            held[pl.ds(k * CHUNK, CHUNK), columns],
            preferred_element_type=jnp.float32,
        )
    pooled_out[...] = pooled
    lab_out[pl.ds(0, 8), :] = lab_low[...]
    lab_out[pl.ds(8, lab_rows), :] = labels[...]
    lab_out[pl.ds(8 + lab_rows, 8), :] = lab_high[...]

    @pl.when(has_high)
    def _():
        for copy in ups:
            copy.wait_send()

    @pl.when(has_low)
    def _():
        for copy in downs:
            copy.wait_send()


def conv_kernel(
    glu, lab_s, lab_v, segs, taps, bn_scale, bn_shift, pooled_frames, w_hbm,
    message, count_message, own, count_out,
    wide, hidden, lab_wide, w_out, mixed, w_sem,
):
    channels = glu.shape[1]
    rows = hidden.shape[0]
    groups = channels // LANES
    kernel = taps.shape[0]
    half = (kernel - 1) // 2
    owned = rows // 32
    me = lax.axis_index("tm")
    column = lax.axis_index("tensor")
    load = pltpu.make_async_copy(w_hbm, w_out, w_sem)
    load.start()

    def widen(start, size):
        block = glu[pl.ds(start, size), :].astype(jnp.float32)
        for g in range(groups):
            wide[g, pl.ds(start, size), :] = block[:, g * LANES : (g + 1) * LANES]

    widen(0, 2 * EDGE)

    def finish(acc, start, g, size):
        lanes = slice(g * LANES, (g + 1) * LANES)
        v = acc * bn_scale[:, lanes] + bn_shift[:, lanes]
        hidden[pl.ds(start, size), lanes] = (v * sigmoid(v)).astype(jnp.bfloat16)

    def step(i, carry):
        base = pl.multiple_of(i * LANES, LANES)
        widen(pl.multiple_of(base + 2 * EDGE, 2 * EDGE), LANES)

        def label(at):
            return lab_s[7 + i + (LANES + at) // LANES, (LANES + at) % LANES]

        @pl.when(label(-half) != label(LANES - 1 + half))
        def _():
            for d in range(3):
                row = lab_v[pl.ds(7 + i + d, 1), :]
                lab_wide[pl.ds(d * LANES, LANES), :] = jnp.transpose(
                    jnp.broadcast_to(row, (LANES, LANES))
                )

        for o in range(0, LANES, SUB):
            same = label(o - half) == label(o + SUB - 1 + half)

            @pl.when(same)
            def _(o=o):
                for g in range(groups):
                    lanes = slice(g * LANES, (g + 1) * LANES)
                    acc = jnp.zeros((SUB, LANES), jnp.float32)
                    for t in range(kernel):
                        x = wide[g, pl.ds(base + (o + t + EDGE - half), SUB), :]
                        acc = acc + taps[t : t + 1, lanes] * x
                    finish(acc, base + o, g, SUB)

            @pl.when(jnp.logical_not(same))
            def _(o=o):
                for p in range(o, o + SUB, 32):
                    center = lab_wide[pl.ds(LANES + p, 32), :]
                    accs = [jnp.zeros((32, LANES), jnp.float32) for _ in range(groups)]
                    for t in range(kernel):
                        keep = lab_wide[pl.ds(LANES + p + t - half, 32), :] == center
                        for g in range(groups):
                            lanes = slice(g * LANES, (g + 1) * LANES)
                            x = wide[g, pl.ds(base + (p + t + EDGE - half), 32), :]
                            accs[g] = accs[g] + taps[t : t + 1, lanes] * jnp.where(keep, x, 0.0)
                    for g in range(groups):
                        finish(accs[g], base + p, g, 32)

        return carry

    lax.fori_loop(0, rows // LANES, step, 0)

    per = CHUNK // LANES
    total = jnp.zeros((2 * owned, channels), jnp.float32)
    tally = jnp.zeros((2 * owned, LANES), jnp.float32)
    for k in range(rows // CHUNK):
        chosen = selection(segs[pl.ds(k * per, per), :] - me * owned, 2 * owned)
        total = total + jnp.dot(
            chosen, hidden[pl.ds(k * CHUNK, CHUNK), :], preferred_element_type=jnp.float32
        )
        wide_chosen = chosen.astype(jnp.float32)
        for q in range(per):
            tally = tally + wide_chosen[:, q * LANES : (q + 1) * LANES]
    count = jnp.broadcast_to(jnp.sum(tally, axis=1, keepdims=True), tally.shape)
    load.wait()
    high = total.astype(jnp.bfloat16)
    low = (total - high.astype(jnp.float32)).astype(jnp.bfloat16)
    mixed[...] = jnp.dot(high, w_out[...], preferred_element_type=jnp.float32) + jnp.dot(
        low, w_out[...], preferred_element_type=jnp.float32
    )
    for j in range(message.shape[1]):
        lanes = slice(j * channels, (j + 1) * channels)
        message[0, j] = mixed[:owned, lanes].astype(jnp.bfloat16)
        message[1, j] = mixed[owned:, lanes].astype(jnp.bfloat16)
    columns = pl.ds(pl.multiple_of(column * channels, LANES), channels)
    mine = mixed[:, columns] + pooled_frames[...]
    own[...] = mine[:owned]
    message[1, column] = mine[owned:].astype(jnp.bfloat16)
    count_out[...] = count[:owned]
    count_message[...] = count[owned:].astype(jnp.bfloat16)


def exchange_kernel(
    tm_count, n, message, count_message, own, count_own, out,
    from_peer, from_behind, from_count, send, recv,
):
    me = lax.axis_index("tm")
    column = lax.axis_index("tensor")
    has_low = me > 0
    has_high = me < tm_count - 1
    others = [lax.rem(column + s, n) for s in range(n)]
    barrier = pltpu.get_barrier_semaphore()
    for s in range(1, n):
        pl.semaphore_signal(
            barrier, inc=1, device_id={"tensor": others[s]}, device_id_type=MESH
        )

    @pl.when(has_low)
    def _():
        for s in range(n):
            pl.semaphore_signal(
                barrier, inc=1, device_id=(me - 1, others[s]), device_id_type=MESH
            )

    @pl.when(has_high)
    def _():
        pl.semaphore_wait(barrier, 2 * n - 1)

    @pl.when(jnp.logical_not(has_high))
    def _():
        pl.semaphore_wait(barrier, n - 1)

    ahead = [
        pltpu.make_async_remote_copy(
            message.at[1, others[s]], from_behind.at[s], send.at[s], recv.at[s],
            device_id=(me + 1, others[s]), device_id_type=MESH,
        )
        for s in range(n)
    ] + [
        pltpu.make_async_remote_copy(
            count_message, from_count, send.at[n], recv.at[n],
            device_id=(me + 1, column), device_id_type=MESH,
        )
    ]
    across = [
        pltpu.make_async_remote_copy(
            message.at[0, others[s]], from_peer.at[s], send.at[n + s], recv.at[n + s],
            device_id=(me, others[s]), device_id_type=MESH,
        )
        for s in range(1, n)
    ]

    @pl.when(has_high)
    def _():
        for copy in ahead:
            copy.start()

    for copy in across:
        copy.start()

    @pl.when(jnp.logical_not(has_low))
    def _():
        from_behind[...] = jnp.zeros(from_behind.shape, from_behind.dtype)
        from_count[...] = jnp.zeros(from_count.shape, from_count.dtype)

    for copy in across:
        copy.wait_recv()

    @pl.when(has_low)
    def _():
        for copy in ahead:
            copy.wait_recv()

    total = own[...]
    for s in range(1, n):
        total = total + from_peer[s].astype(jnp.float32)
    for s in range(n):
        total = total + from_behind[s].astype(jnp.float32)
    count = count_own[...] + from_count[...].astype(jnp.float32)
    for g in range(out.shape[1] // LANES):
        lanes = slice(g * LANES, (g + 1) * LANES)
        out[:, lanes] = total[:, lanes] / count
    for copy in across:
        copy.wait_send()

    @pl.when(has_high)
    def _():
        for copy in ahead:
            copy.wait_send()


def shards(
    tm_count, n,
    frames, utt_ids, seg_ids, norm_gain, w_value, w_gate, conv_taps, bn_scale, bn_shift, w_out
):
    rows, width = frames.shape
    channels = w_value.shape[1]
    owned = rows // 32
    lab_rows = rows // LANES
    bf16, f32, i32 = jnp.bfloat16, jnp.float32, jnp.int32
    shape = jax.ShapeDtypeStruct
    dma = pltpu.SemaphoreType.DMA
    labels = utt_ids.reshape(lab_rows, LANES)
    segs = seg_ids.reshape(lab_rows, LANES)
    glu, lab, pooled = pl.pallas_call(
        functools.partial(glu_kernel, tm_count),
        name="glu",
        out_shape=[
            shape((rows + 2 * EDGE, channels), bf16),
            shape((lab_rows + 16, LANES), i32),
            shape((2 * owned, channels), f32),
        ],
        in_specs=[HBM, VMEM, VMEM, VMEM, HBM, HBM],
        out_specs=[VMEM, VMEM, VMEM],
        scratch_shapes=[
            pltpu.VMEM((rows, width), bf16),
            pltpu.VMEM((2, CHUNK + 2 * EDGE, width), bf16),
            pltpu.VMEM((2 * EDGE, width), bf16),
            pltpu.VMEM((8, LANES), i32),
            pltpu.VMEM((8, LANES), i32),
            pltpu.VMEM((width, channels), bf16),
            pltpu.VMEM((width, channels), bf16),
            dma((rows // CHUNK,)),
            dma((2,)),
            dma((4,)),
            dma((4,)),
        ],
        compiler_params=pltpu.CompilerParams(
            collective_id=0, has_side_effects=True, vmem_limit_bytes=61 * MIB
        ),
    )(frames, labels, segs, norm_gain.reshape(1, width), w_value, w_gate)
    message, count_message, own, count = pl.pallas_call(
        conv_kernel,
        name="conv",
        out_shape=[
            shape((2, n, owned, channels), bf16),
            shape((owned, LANES), bf16),
            shape((owned, channels), f32),
            shape((owned, LANES), f32),
        ],
        in_specs=[VMEM, pl.BlockSpec(memory_space=pltpu.SMEM)] + [VMEM] * 6 + [HBM],
        out_specs=[VMEM] * 4,
        scratch_shapes=[
            pltpu.VMEM((channels // LANES, rows + 2 * EDGE, LANES), f32),
            pltpu.VMEM((rows, channels), bf16),
            pltpu.VMEM((3 * LANES, LANES), i32),
            pltpu.VMEM(w_out.shape, bf16),
            pltpu.VMEM((2 * owned, w_out.shape[1]), f32),
            dma(()),
        ],
        compiler_params=pltpu.CompilerParams(vmem_limit_bytes=32 * MIB),
    )(
        glu, lab, lab, segs, conv_taps, bn_scale.reshape(1, channels),
        bn_shift.reshape(1, channels), pooled, w_out,
    )
    return pl.pallas_call(
        functools.partial(exchange_kernel, tm_count, n),
        name="exchange",
        out_shape=shape((owned, channels), f32),
        in_specs=[VMEM] * 4,
        out_specs=VMEM,
        scratch_shapes=[
            pltpu.VMEM((n, owned, channels), bf16),
            pltpu.VMEM((n, owned, channels), bf16),
            pltpu.VMEM((owned, LANES), bf16),
            dma((2 * n,)),
            dma((2 * n,)),
        ],
        compiler_params=pltpu.CompilerParams(
            collective_id=1, has_side_effects=True, vmem_limit_bytes=8 * MIB
        ),
    )(message, count_message, own, count)


def solution(mesh):
    in_specs = (
        P("tm", None),
        P("tm"),
        P("tm"),
        P(),
        P(None, "tensor"),
        P(None, "tensor"),
        P(None, "tensor"),
        P("tensor"),
        P("tensor"),
        P("tensor", None),
    )
    out_specs = P("tm", "tensor")
    body = functools.partial(shards, mesh.shape["tm"], mesh.shape["tensor"])
    return jax.shard_map(body, mesh=mesh, in_specs=in_specs, out_specs=out_specs, check_vma=False)
```

time: 98.4 us -> 39 us (0.40); the launches traced: 96.8 us -> 39 us
  matrix products: 41.7 us -> 0 us
  Pallas kernels: 0 us -> 34.9 us
  starting transfers between devices: 19.9 us -> 0 us
  waiting for transfers between devices: 13.8 us -> 0 us
  between operations: 13.8 us -> 0.09 us
  other arithmetic: 6.73 us -> 0 us
  local copies, waits for them, and re-layouts: 0.83 us -> 3.94 us
    dot_general x5 -> x0, matrix products: 41.7 us -> none  [the longest x1 32 us: shards(): jnp.dot(onehot, hidden, preferred_element_type=jnp.float32)]
    pallas_call x0 -> x3, Pallas kernels: none -> 34.9 us  [the longest x1 15 us: shards(): pl.pallas_call(conv_kernel, name='conv', out_shape=[shape((2, n, owned, c...]
    ppermute x6 -> x0, starting transfers between devices: 19.9 us -> none  [the longest x2 9.95 us: padded_2(): lax.ppermute(lax.slice_in_dim(block, 0, width, axis=dim), axis, backward)]
    reduce_scatter x1 -> x0, waiting for transfers between devices: 8.02 us -> none  [shards(): lax.psum_scatter(partial_value.astype(jnp.bfloat16), 'tensor', scatter_di...]
    ppermute x6 -> x0, waiting for transfers between devices: 5.77 us -> none  [the longest x2 5.76 us: from_behind(): lax.ppermute(value, axis, [(source, source + steps) for source in range(l...]
    reduce_sum x3 -> x0, other arithmetic: 4.53 us -> none  [the longest x1 2.95 us: shards(): center = jnp.mean(floats, axis=1, keepdims=True)]
    unnamed x20 -> x17, local copies, waits for them, and re-layouts: 0.62 us -> 3.94 us
    add x2 -> x0, other arithmetic: 1.51 us -> none  [the longest x1 1.51 us: shards(): return mean_frames + mixed]
  transfers between devices with their start and end apart: 7 -> 0, of which waited for: 2 -> 0; matrix products, arithmetic and copies ran while one was open for 36% -> 0% of each run, Pallas kernels for 0% -> 0%
where the time goes in v1:
time: 39 us
  Pallas kernels  34.9 us (89%)
  local copies, waits for them, and re-layouts  3.94 us (10%)
    pallas_call x1, Pallas kernels, shards(): pl.pallas_call(conv_kernel, name='conv', out_shape=[shape((2, n, owned, c...  15 us
    pallas_call x1, Pallas kernels, shards(): pl.pallas_call(functools.partial(glu_kernel, tm_count), name='glu', out_s...  11.8 us
    pallas_call x1, Pallas kernels, shards(): pl.pallas_call(functools.partial(exchange_kernel, tm_count, n), name='exc...  8.12 us
    unnamed x17, local copies, waits for them, and re-layouts  3.94 us

profile of v1, /device:TPU:8, one launch (start us, length us, event | category | flops | bytes accessed | tf_op | source)
XLA Modules:
  0.0 39.0 jit_solution(9299899520401607640)
XLA Ops:
  0.0 0.0 copy-start.1
  0.0 0.0 copy-start.7
  0.0 0.0 copy-start.6
  0.0 0.0 copy-start.4
  0.0 0.0 copy-start.5
  0.0 11.8 %glu.1 = (bf16[2080,512]{1,0:T(8,128)(2,1)}, s32[32,128]{1,0:T(8,128)}, f32[128,512]{1,0:T(8,128)}) custom-call(bf16[2048,1024]{1,0:T(8,128)(2,1)} %frames.1, s32[16,128]{1,0:T(8,128)} %bitcast.9, s32[16,128]{1,0:T(8,128)} %bitcast.5, f32[1,1024]{1,0:T(1,128)} %bitcast.10, bf16[1024,512]{1,0:T(8,128)(2,1)} %wv_hbm.1, bf16[1024,512]{1,0:T(8,128)(2,1)} %wg_hbm.1), custom_call_target="tpu_custom_call" | custom-call | tf_op jit(solution)/shard_map/glu/pallas_call | solution.py:396
  11.9 0.0 copy-done.1
  11.9 0.0 copy-done.7
  11.9 0.0 copy-done.6
  11.9 0.0 copy-done.4
  11.9 0.0 copy-done.5
  11.9 0.0 copy-start
  11.9 1.6 %copy-done = bf16[2080,512]{1,0:T(8,128)(2,1)S(1)} copy-done((bf16[2080,512]{1,0:T(8,128)(2,1)S(1)}, bf16[2080,512]{1,0:T(8,128)(2,1)}, u32[]{:S(2)}) %copy-start) | copy-done | bytes 2129944
  13.5 0.0 copy-start.2
  13.5 0.9 %copy-done.2 = f32[128,512]{1,0:T(8,128)S(1)} copy-done((f32[128,512]{1,0:T(8,128)S(1)}, f32[128,512]{1,0:T(8,128)}, u32[]{:S(2)}) %copy-start.2) | copy-done | bytes 262168
  14.5 0.0 copy-start.3
  14.5 0.7 %copy-done.3 = s32[32,128]{1,0:T(8,128)S(1)} copy-done((s32[32,128]{1,0:T(8,128)S(1)}, s32[32,128]{1,0:T(8,128)}, u32[]{:S(2)}) %copy-start.3) | copy-done | bytes 16408
  15.2 15.0 %conv.1 = (bf16[2,2,64,512]{3,2,1,0:T(8,128)(2,1)S(1)}, bf16[64,128]{1,0:T(8,128)(2,1)S(1)}, f32[64,512]{1,0:T(8,128)S(1)}, f32[64,128]{1,0:T(8,128)S(1)}) custom-call(bf16[2080,512]{1,0:T(8,128)(2,1)S(1)} %copy-done, s32[32,128]{1,0:T(8,128)S(1)} %copy-done.3, s32[32,128]{1,0:T(8,128)S(1)} %copy-done.3, s32[16,128]{1,0:T(8,128)S(1)} %bitcast.6, ...), custom_call_target="tpu_custom_call" | custom-call | tf_op jit(solution)/shard_map/conv/pallas_call | solution.py:423
  30.2 8.1 %exchange.1 = f32[64,512]{1,0:T(8,128)S(1)} custom-call(bf16[2,2,64,512]{3,2,1,0:T(8,128)(2,1)S(1)} %get-tuple-element.15.message, bf16[64,128]{1,0:T(8,128)(2,1)S(1)} %get-tuple-element.16.count_message, f32[64,512]{1,0:T(8,128)S(1)} %get-tuple-element.17.own, f32[64,128]{1,0:T(8,128)S(1)} %get-tuple-element.18.count_own), custom_call_target="tpu_custom_call" | custom-call | tf_op jit(solution)/shard_map/exchange/pallas_call | solution.py:447
  38.3 0.7 %copy.12 = f32[64,512]{1,0:T(8,128)} copy(f32[64,512]{1,0:T(8,128)S(1)} %exchange.1) | data formatting | bytes 262144
Async XLA Ops:
  0.0 11.9 %copy-start.1 = (bf16[512,1024]{1,0:T(8,128)(2,1)S(1)}, bf16[512,1024]{1,0:T(8,128)(2,1)}, u32[]{:S(2)}) copy-start(bf16[512,1024]{1,0:T(8,128)(2,1)} %w_hbm.1) | copy-start | bytes 3145732
  0.0 11.9 %copy-start.7 = (f32[512]{0:T(512)S(1)}, f32[512]{0:T(512)}, u32[]{:S(2)}) copy-start(f32[512]{0:T(512)} %param.18) | copy-start | bytes 6148
  0.0 11.9 %copy-start.6 = (f32[512]{0:T(512)S(1)}, f32[512]{0:T(512)}, u32[]{:S(2)}) copy-start(f32[512]{0:T(512)} %param.17) | copy-start | bytes 6148
  0.0 11.9 %copy-start.4 = (f32[31,512]{1,0:T(8,128)S(1)}, f32[31,512]{1,0:T(8,128)}, u32[]{:S(2)}) copy-start(f32[31,512]{1,0:T(8,128)} %taps.1) | copy-start | bytes 190468
  0.0 11.9 %copy-start.5 = (s32[2048]{0:T(1024)S(1)}, s32[2048]{0:T(1024)}, u32[]{:S(2)}) copy-start(s32[2048]{0:T(1024)} %param.12) | copy-start | bytes 24580
  11.9 1.6 %copy-start = (bf16[2080,512]{1,0:T(8,128)(2,1)S(1)}, bf16[2080,512]{1,0:T(8,128)(2,1)}, u32[]{:S(2)}) copy-start(bf16[2080,512]{1,0:T(8,128)(2,1)} %get-tuple-element.12.glu) | copy-start | bytes 6389764
  13.5 0.9 %copy-start.2 = (f32[128,512]{1,0:T(8,128)S(1)}, f32[128,512]{1,0:T(8,128)}, u32[]{:S(2)}) copy-start(f32[128,512]{1,0:T(8,128)} %get-tuple-element.14.pooled_frames) | copy-start | bytes 786436
  14.5 0.7 %copy-start.3 = (s32[32,128]{1,0:T(8,128)S(1)}, s32[32,128]{1,0:T(8,128)}, u32[]{:S(2)}) copy-start(s32[32,128]{1,0:T(8,128)} %get-tuple-element.13.lab_s.lab_v) | copy-start | bytes 49156

commit v2 on v1

--- a/solution.py
+++ b/solution.py
@@ -41,7 +41,7 @@
 def glu_kernel(
     tm_count, frames, labels, segs, gain, wv_hbm, wg_hbm,
     glu_out, lab_out, pooled_out,
-    held, normed, halo, lab_low, lab_high, wv, wg, chunk_sems, w_sems, send, recv,
+    held, normed, halo, lab_low, lab_high, wv, wg, made, chunk_sems, w_sems, send, recv, out_sems,
 ):
     rows = frames.shape[0]
     channels = wv.shape[1]
@@ -132,18 +132,33 @@
     per = CHUNK // LANES
     pooled = jnp.zeros((2 * owned, channels), jnp.float32)
 
-    def prepare(k):
-        loads[k].wait()
-        normed[k % 2, pl.ds(0, CHUNK), :] = normalised(held[pl.ds(k * CHUNK, CHUNK), :], scale)
-
-    prepare(0)
+    width = min(channels, 256)
+    slices = channels // width
+    part = CHUNK // slices
+
+    def prepare(k, j):
+        normed[k % 2, pl.ds(j * part, part), :] = normalised(
+            held[pl.ds(k * CHUNK + j * part, part), :], scale
+        )
+
+    def store(start, size, sem):
+        here = pl.ds(start, size)
+        return pltpu.make_async_copy(made.at[here], glu_out.at[here], out_sems.at[sem])
+
+    stores = [store(EDGE + k * CHUNK, CHUNK, k) for k in range(chunks - 1)]
+    stores.append(store(EDGE + rows - CHUNK, CHUNK + EDGE, chunks - 1))
+    stores.append(store(0, EDGE, chunks))
+
+    loads[0].wait()
+    for j in range(slices):
+        prepare(0, j)
     for copy in weights:
         copy.wait()
     for k in range(chunks):
+        size = CHUNK
         if k + 1 < chunks:
-            prepare(k + 1)
-        size = CHUNK
-        if k == chunks - 1:
+            loads[k + 1].wait()
+        else:
             size = CHUNK + 2 * EDGE
 
             @pl.when(has_low)
@@ -158,13 +173,20 @@
 
             normed[k % 2, pl.ds(CHUNK, 2 * EDGE), :] = normalised(halo[...], scale)
         block = normed[k % 2, pl.ds(0, size), :]
-        value = jnp.dot(block, wv[...], preferred_element_type=jnp.float32)
-        gate = jnp.dot(block, wg[...], preferred_element_type=jnp.float32)
-        glu = (value * sigmoid(gate)).astype(jnp.bfloat16)
-        glu_out[pl.ds(EDGE + k * CHUNK, CHUNK), :] = glu[:CHUNK]
+        for j in range(slices):
+            lanes = slice(j * width, (j + 1) * width)
+            value = jnp.dot(block, wv[:, lanes], preferred_element_type=jnp.float32)
+            gate = jnp.dot(block, wg[:, lanes], preferred_element_type=jnp.float32)
+            if k + 1 < chunks:
+                prepare(k + 1, j)
+            glu = (value * sigmoid(gate)).astype(jnp.bfloat16)
+            made[pl.ds(EDGE + k * CHUNK, CHUNK), lanes] = glu[:CHUNK]
+            if k == chunks - 1:
+                made[pl.ds(0, EDGE), lanes] = glu[CHUNK : CHUNK + EDGE]
+                made[pl.ds(EDGE + rows, EDGE), lanes] = glu[CHUNK + EDGE :]
+        stores[k].start()
         if k == chunks - 1:
-            glu_out[pl.ds(0, EDGE), :] = glu[CHUNK : CHUNK + EDGE]
-            glu_out[pl.ds(EDGE + rows, EDGE), :] = glu[CHUNK + EDGE :]
+            stores[k + 1].start()
         slots = segs[pl.ds(k * per, per), :] - me * owned
         pooled = pooled + jnp.dot(
             selection(slots, 2 * owned),
@@ -175,6 +197,8 @@
     lab_out[pl.ds(0, 8), :] = lab_low[...]
     lab_out[pl.ds(8, lab_rows), :] = labels[...]
     lab_out[pl.ds(8 + lab_rows, 8), :] = lab_high[...]
+    for copy in stores:
+        copy.wait()
 
     @pl.when(has_high)
     def _():
@@ -188,9 +212,9 @@
 
 
 def conv_kernel(
-    glu, lab_s, lab_v, segs, taps, bn_scale, bn_shift, pooled_frames, w_hbm,
+    glu_hbm, lab_s, lab_v, segs, taps, bn_scale, bn_shift, pooled_hbm, w_hbm,
     message, count_message, own, count_out,
-    wide, hidden, lab_wide, w_out, mixed, w_sem,
+    wide, hidden, lab_wide, w_out, mixed, glu, pooled_frames, sems, glu_sems,
 ):
     channels = glu.shape[1]
     rows = hidden.shape[0]
@@ -200,8 +224,22 @@
     owned = rows // 32
     me = lax.axis_index("tm")
     column = lax.axis_index("tensor")
-    load = pltpu.make_async_copy(w_hbm, w_out, w_sem)
-    load.start()
+
+    def piece(start, size, k):
+        here = pl.ds(start, size)
+        return pltpu.make_async_copy(glu_hbm.at[here], glu.at[here], glu_sems.at[k])
+
+    first = piece(0, CHUNK + 2 * EDGE, 0)
+    first.start()
+    for k in range(1, rows // CHUNK):
+        piece(k * CHUNK + 2 * EDGE, CHUNK, k).start()
+    late = [
+        pltpu.make_async_copy(w_hbm, w_out, sems.at[0]),
+        pltpu.make_async_copy(pooled_hbm, pooled_frames, sems.at[1]),
+    ]
+    for copy in late:
+        copy.start()
+    first.wait()
 
     def widen(start, size):
         block = glu[pl.ds(start, size), :].astype(jnp.float32)
@@ -217,6 +255,12 @@
 
     def step(i, carry):
         base = pl.multiple_of(i * LANES, LANES)
+        k = i // (CHUNK // LANES)
+
+        @pl.when(jnp.logical_and(i > 0, k * (CHUNK // LANES) == i))
+        def _():
+            piece(pl.multiple_of(k * CHUNK + 2 * EDGE, 2 * EDGE), CHUNK, k).wait()
+
         widen(pl.multiple_of(base + 2 * EDGE, 2 * EDGE), LANES)
 
         def label(at):
@@ -273,11 +317,10 @@
         for q in range(per):
             tally = tally + wide_chosen[:, q * LANES : (q + 1) * LANES]
     count = jnp.broadcast_to(jnp.sum(tally, axis=1, keepdims=True), tally.shape)
-    load.wait()
-    high = total.astype(jnp.bfloat16)
-    low = (total - high.astype(jnp.float32)).astype(jnp.bfloat16)
-    mixed[...] = jnp.dot(high, w_out[...], preferred_element_type=jnp.float32) + jnp.dot(
-        low, w_out[...], preferred_element_type=jnp.float32
+    for copy in late:
+        copy.wait()
+    mixed[...] = jnp.dot(
+        total.astype(jnp.bfloat16), w_out[...], preferred_element_type=jnp.float32
     )
     for j in range(message.shape[1]):
         lanes = slice(j * channels, (j + 1) * channels)
@@ -402,7 +445,7 @@
             shape((2 * owned, channels), f32),
         ],
         in_specs=[HBM, VMEM, VMEM, VMEM, HBM, HBM],
-        out_specs=[VMEM, VMEM, VMEM],
+        out_specs=[HBM, VMEM, VMEM],
         scratch_shapes=[
             pltpu.VMEM((rows, width), bf16),
             pltpu.VMEM((2, CHUNK + 2 * EDGE, width), bf16),
@@ -411,13 +454,15 @@
             pltpu.VMEM((8, LANES), i32),
             pltpu.VMEM((width, channels), bf16),
             pltpu.VMEM((width, channels), bf16),
+            pltpu.VMEM((rows + 2 * EDGE, channels), bf16),
             dma((rows // CHUNK,)),
             dma((2,)),
             dma((4,)),
             dma((4,)),
+            dma((rows // CHUNK + 1,)),
         ],
         compiler_params=pltpu.CompilerParams(
-            collective_id=0, has_side_effects=True, vmem_limit_bytes=61 * MIB
+            collective_id=0, has_side_effects=True, vmem_limit_bytes=60 * MIB
         ),
     )(frames, labels, segs, norm_gain.reshape(1, width), w_value, w_gate)
     message, count_message, own, count = pl.pallas_call(
@@ -429,7 +474,7 @@
             shape((owned, channels), f32),
             shape((owned, LANES), f32),
         ],
-        in_specs=[VMEM, pl.BlockSpec(memory_space=pltpu.SMEM)] + [VMEM] * 6 + [HBM],
+        in_specs=[HBM, pl.BlockSpec(memory_space=pltpu.SMEM)] + [VMEM] * 5 + [HBM, HBM],
         out_specs=[VMEM] * 4,
         scratch_shapes=[
             pltpu.VMEM((channels // LANES, rows + 2 * EDGE, LANES), f32),
@@ -437,9 +482,12 @@
             pltpu.VMEM((3 * LANES, LANES), i32),
             pltpu.VMEM(w_out.shape, bf16),
             pltpu.VMEM((2 * owned, w_out.shape[1]), f32),
-            dma(()),
+            pltpu.VMEM((rows + 2 * EDGE, channels), bf16),
+            pltpu.VMEM((2 * owned, channels), f32),
+            dma((2,)),
+            dma((rows // CHUNK,)),
         ],
-        compiler_params=pltpu.CompilerParams(vmem_limit_bytes=32 * MIB),
+        compiler_params=pltpu.CompilerParams(vmem_limit_bytes=60 * MIB),
     )(
         glu, lab, lab, segs, conv_taps, bn_scale.reshape(1, channels),
         bn_shift.reshape(1, channels), pooled, w_out,
@@ -448,7 +496,7 @@
         functools.partial(exchange_kernel, tm_count, n),
         name="exchange",
         out_shape=shape((owned, channels), f32),
-        in_specs=[VMEM] * 4,
+        in_specs=[HBM] + [VMEM] * 3,
         out_specs=VMEM,
         scratch_shapes=[
             pltpu.VMEM((n, owned, channels), bf16),
@@ -458,7 +506,7 @@
             dma((2 * n,)),
         ],
         compiler_params=pltpu.CompilerParams(
-            collective_id=1, has_side_effects=True, vmem_limit_bytes=8 * MIB
+            collective_id=1, has_side_effects=True, vmem_limit_bytes=60 * MIB
         ),
     )(message, count_message, own, count)
 

time: 39 us -> 40.4 us (1.036)
  Pallas kernels: 34.9 us -> 38.5 us
  local copies, waits for them, and re-layouts: 3.94 us -> 1.57 us
    unnamed x17 -> x1, local copies, waits for them, and re-layouts: 3.94 us -> 1.57 us
    pallas_call x1, Pallas kernels: 15 us -> 17.1 us  [shards(): pl.pallas_call(conv_kernel, name='conv', out_shape=[shape((2, n, owned, c...]
    pallas_call x1, Pallas kernels: 8.12 us -> 9.85 us  [shards(): pl.pallas_call(functools.partial(exchange_kernel, tm_count, n), name='exc...]
where the time goes in v2:
time: 40.4 us; the launch traced here: 40.1 us
  Pallas kernels  38.5 us (95%)
  local copies, waits for them, and re-layouts  1.57 us (4%)
    pallas_call x1, Pallas kernels, shards(): pl.pallas_call(conv_kernel, name='conv', out_shape=[shape((2, n, owned, c...  17.1 us
    pallas_call x1, Pallas kernels, shards(): pl.pallas_call(functools.partial(glu_kernel, tm_count), name='glu', out_s...  11.6 us
    pallas_call x1, Pallas kernels, shards(): pl.pallas_call(functools.partial(exchange_kernel, tm_count, n), name='exc...  9.85 us
    unnamed x1, local copies, waits for them, and re-layouts  1.57 us

profile of v2, /device:TPU:8, one launch (start us, length us, event | category | flops | bytes accessed | tf_op | source)
XLA Modules:
  0.0 40.1 jit_solution(16437961356520816912)
XLA Ops:
  0.0 11.6 %glu.1 = (bf16[2080,512]{1,0:T(8,128)(2,1)}, s32[32,128]{1,0:T(8,128)}, f32[128,512]{1,0:T(8,128)}) custom-call(bf16[2048,1024]{1,0:T(8,128)(2,1)} %frames.1, s32[16,128]{1,0:T(8,128)} %bitcast.7, s32[16,128]{1,0:T(8,128)} %bitcast.5, f32[1,1024]{1,0:T(1,128)} %bitcast.8, bf16[1024,512]{1,0:T(8,128)(2,1)} %wv_hbm.1, bf16[1024,512]{1,0:T(8,128)(2,1)} %wg_hbm.1), custom_call_target="tpu_custom_call" | custom-call | tf_op jit(solution)/shard_map/glu/pallas_call | solution.py:439
  11.6 17.1 %conv.1 = (bf16[2,2,64,512]{3,2,1,0:T(8,128)(2,1)}, bf16[64,128]{1,0:T(8,128)(2,1)}, f32[64,512]{1,0:T(8,128)}, f32[64,128]{1,0:T(8,128)}) custom-call(bf16[2080,512]{1,0:T(8,128)(2,1)} %get-tuple-element.12.glu_hbm, s32[32,128]{1,0:T(8,128)} %get-tuple-element.13.lab_s.lab_v, s32[32,128]{1,0:T(8,128)} %get-tuple-element.13.lab_s.lab_v, s32[16,128]{1,0:T(8,128)} %bitcast.6, ...), custom_call_target="tpu_custom_call" | custom-call | tf_op jit(solution)/shard_map/conv/pallas_call | solution.py:468
  28.7 9.8 %exchange.1 = f32[64,512]{1,0:T(8,128)} custom-call(bf16[2,2,64,512]{3,2,1,0:T(8,128)(2,1)} %get-tuple-element.15.message, bf16[64,128]{1,0:T(8,128)(2,1)} %get-tuple-element.16.count_message, f32[64,512]{1,0:T(8,128)} %get-tuple-element.17.own, f32[64,128]{1,0:T(8,128)} %get-tuple-element.18.count_own), custom_call_target="tpu_custom_call" | custom-call | tf_op jit(solution)/shard_map/exchange/pallas_call | solution.py:495
  38.5 1.6 %copy.12 = f32[64,512]{1,0:T(8,128)} copy(f32[64,512]{1,0:T(8,128)} %exchange.1) | data formatting | bytes 262144

commit v3 on v2

--- a/solution.py
+++ b/solution.py
@@ -13,7 +13,7 @@
 EDGE = 16
 LANES = 128
 CHUNK = 256
-SUB = 64
+SUB = 32
 MIB = 1 << 20
 
 
@@ -266,40 +266,44 @@
         def label(at):
             return lab_s[7 + i + (LANES + at) // LANES, (LANES + at) % LANES]
 
-        @pl.when(label(-half) != label(LANES - 1 + half))
+        def plain(o, size):
+            for g in range(groups):
+                lanes = slice(g * LANES, (g + 1) * LANES)
+                acc = jnp.zeros((size, LANES), jnp.float32)
+                for t in range(kernel):
+                    x = wide[g, pl.ds(base + (o + t + EDGE - half), size), :]
+                    acc = acc + taps[t : t + 1, lanes] * x
+                finish(acc, base + o, g, size)
+
+        def masked(o, size):
+            center = lab_wide[pl.ds(LANES + o, size), :]
+            accs = [jnp.zeros((size, LANES), jnp.float32) for _ in range(groups)]
+            for t in range(kernel):
+                keep = lab_wide[pl.ds(LANES + o + t - half, size), :] == center
+                for g in range(groups):
+                    lanes = slice(g * LANES, (g + 1) * LANES)
+                    x = wide[g, pl.ds(base + (o + t + EDGE - half), size), :]
+                    accs[g] = accs[g] + taps[t : t + 1, lanes] * jnp.where(keep, x, 0.0)
+            for g in range(groups):
+                finish(accs[g], base + o, g, size)
+
+        whole = label(-half) == label(LANES - 1 + half)
+
+        @pl.when(whole)
+        def _():
+            plain(0, LANES)
+
+        @pl.when(jnp.logical_not(whole))
         def _():
             for d in range(3):
                 row = lab_v[pl.ds(7 + i + d, 1), :]
                 lab_wide[pl.ds(d * LANES, LANES), :] = jnp.transpose(
                     jnp.broadcast_to(row, (LANES, LANES))
                 )
-
-        for o in range(0, LANES, SUB):
-            same = label(o - half) == label(o + SUB - 1 + half)
-
-            @pl.when(same)
-            def _(o=o):
-                for g in range(groups):
-                    lanes = slice(g * LANES, (g + 1) * LANES)
-                    acc = jnp.zeros((SUB, LANES), jnp.float32)
-                    for t in range(kernel):
-                        x = wide[g, pl.ds(base + (o + t + EDGE - half), SUB), :]
-                        acc = acc + taps[t : t + 1, lanes] * x
-                    finish(acc, base + o, g, SUB)
-
-            @pl.when(jnp.logical_not(same))
-            def _(o=o):
-                for p in range(o, o + SUB, 32):
-                    center = lab_wide[pl.ds(LANES + p, 32), :]
-                    accs = [jnp.zeros((32, LANES), jnp.float32) for _ in range(groups)]
-                    for t in range(kernel):
-                        keep = lab_wide[pl.ds(LANES + p + t - half, 32), :] == center
-                        for g in range(groups):
-                            lanes = slice(g * LANES, (g + 1) * LANES)
-                            x = wide[g, pl.ds(base + (p + t + EDGE - half), 32), :]
-                            accs[g] = accs[g] + taps[t : t + 1, lanes] * jnp.where(keep, x, 0.0)
-                    for g in range(groups):
-                        finish(accs[g], base + p, g, 32)
+            for o in range(0, LANES, SUB):
+                same = label(o - half) == label(o + SUB - 1 + half)
+                pl.when(same)(functools.partial(plain, o, SUB))
+                pl.when(jnp.logical_not(same))(functools.partial(masked, o, SUB))
 
         return carry
 
@@ -462,7 +466,7 @@
             dma((rows // CHUNK + 1,)),
         ],
         compiler_params=pltpu.CompilerParams(
-            collective_id=0, has_side_effects=True, vmem_limit_bytes=60 * MIB
+            collective_id=0, has_side_effects=True, vmem_limit_bytes=53 * MIB
         ),
     )(frames, labels, segs, norm_gain.reshape(1, width), w_value, w_gate)
     message, count_message, own, count = pl.pallas_call(
@@ -487,7 +491,7 @@
             dma((2,)),
             dma((rows // CHUNK,)),
         ],
-        compiler_params=pltpu.CompilerParams(vmem_limit_bytes=60 * MIB),
+        compiler_params=pltpu.CompilerParams(vmem_limit_bytes=53 * MIB),
     )(
         glu, lab, lab, segs, conv_taps, bn_scale.reshape(1, channels),
         bn_shift.reshape(1, channels), pooled, w_out,
@@ -496,7 +500,7 @@
         functools.partial(exchange_kernel, tm_count, n),
         name="exchange",
         out_shape=shape((owned, channels), f32),
-        in_specs=[HBM] + [VMEM] * 3,
+        in_specs=[VMEM] * 4,
         out_specs=VMEM,
         scratch_shapes=[
             pltpu.VMEM((n, owned, channels), bf16),
@@ -506,7 +510,7 @@
             dma((2 * n,)),
         ],
         compiler_params=pltpu.CompilerParams(
-            collective_id=1, has_side_effects=True, vmem_limit_bytes=60 * MIB
+            collective_id=1, has_side_effects=True, vmem_limit_bytes=8 * MIB
         ),
     )(message, count_message, own, count)
 

time: 40.4 us -> 37.4 us (0.926)
  Pallas kernels: 38.5 us -> 34.2 us
  local copies, waits for them, and re-layouts: 1.57 us -> 2.78 us
    pallas_call x1, Pallas kernels: 9.85 us -> 8.12 us  [shards(): pl.pallas_call(functools.partial(exchange_kernel, tm_count, n), name='exc...]
    pallas_call x1, Pallas kernels: 11.6 us -> 10.2 us  [shards(): pl.pallas_call(functools.partial(glu_kernel, tm_count), name='glu', out_s...]
    unnamed x1 -> x13, local copies, waits for them, and re-layouts: 1.57 us -> 2.78 us
    pallas_call x1, Pallas kernels: 17.1 us -> 15.9 us  [shards(): pl.pallas_call(conv_kernel, name='conv', out_shape=[shape((2, n, owned, c...]
where the time goes in v3:
time: 37.4 us; the launch traced here: 37 us
  Pallas kernels  34.2 us (91%)
  local copies, waits for them, and re-layouts  2.78 us (7%)
    pallas_call x1, Pallas kernels, shards(): pl.pallas_call(conv_kernel, name='conv', out_shape=[shape((2, n, owned, c...  15.9 us
    pallas_call x1, Pallas kernels, shards(): pl.pallas_call(functools.partial(glu_kernel, tm_count), name='glu', out_s...  10.2 us
    pallas_call x1, Pallas kernels, shards(): pl.pallas_call(functools.partial(exchange_kernel, tm_count, n), name='exc...  8.12 us
    unnamed x13, local copies, waits for them, and re-layouts  2.78 us

profile of v3, /device:TPU:8, one launch (start us, length us, event | category | flops | bytes accessed | tf_op | source)
XLA Modules:
  0.0 37.0 jit_solution(14718802047104307829)
XLA Ops:
  0.0 0.0 copy-start
  0.0 0.0 copy-start.1
  0.0 0.7 %copy-done.1 = s32[2048]{0:T(1024)S(1)} copy-done((s32[2048]{0:T(1024)S(1)}, s32[2048]{0:T(1024)}, u32[]{:S(2)}) %copy-start.1) | copy-done | bytes 8216
  0.7 0.0 copy-start.2
  0.7 0.7 %copy-done.2 = s32[2048]{0:T(1024)S(1)} copy-done((s32[2048]{0:T(1024)S(1)}, s32[2048]{0:T(1024)}, u32[]{:S(2)}) %copy-start.2) | copy-done | bytes 8216
  1.4 0.0 copy-start.3
  1.4 0.7 %copy-done.3 = f32[1024]{0:T(1024)S(1)} copy-done((f32[1024]{0:T(1024)S(1)}, f32[1024]{0:T(1024)}, u32[]{:S(2)}) %copy-start.3) | copy-done | bytes 4120
  2.1 0.0 copy-start.4
  2.1 0.0 copy-start.5
  2.1 10.2 %glu.1 = (bf16[2080,512]{1,0:T(8,128)(2,1)}, s32[32,128]{1,0:T(8,128)S(1)}, f32[128,512]{1,0:T(8,128)S(1)}) custom-call(bf16[2048,1024]{1,0:T(8,128)(2,1)} %frames.1, s32[16,128]{1,0:T(8,128)S(1)} %bitcast.7, s32[16,128]{1,0:T(8,128)S(1)} %bitcast.5, f32[1,1024]{1,0:T(1,128)S(1)} %bitcast.8, bf16[1024,512]{1,0:T(8,128)(2,1)} %wv_hbm.1, bf16[1024,512]{1,0:T(8,128)(2,1)} %wg_hbm.1), custom_call_target="tpu_custom_call" | custom-call | tf_op jit(solution)/shard_map/glu/pallas_call | solution.py:443
  12.3 0.0 copy-done
  12.3 0.0 copy-done.4
  12.3 0.0 copy-done.5
  12.3 15.9 %conv.1 = (bf16[2,2,64,512]{3,2,1,0:T(8,128)(2,1)S(1)}, bf16[64,128]{1,0:T(8,128)(2,1)S(1)}, f32[64,512]{1,0:T(8,128)S(1)}, f32[64,128]{1,0:T(8,128)S(1)}) custom-call(bf16[2080,512]{1,0:T(8,128)(2,1)} %get-tuple-element.12.glu_hbm, s32[32,128]{1,0:T(8,128)S(1)} %get-tuple-element.13.lab_s.lab_v, s32[32,128]{1,0:T(8,128)S(1)} %get-tuple-element.13.lab_s.lab_v, ...), custom_call_target="tpu_custom_call" | custom-call | tf_op jit(solution)/shard_map/conv/pallas_call | solution.py:472
  28.3 8.1 %exchange.1 = f32[64,512]{1,0:T(8,128)S(1)} custom-call(bf16[2,2,64,512]{3,2,1,0:T(8,128)(2,1)S(1)} %get-tuple-element.15.message, bf16[64,128]{1,0:T(8,128)(2,1)S(1)} %get-tuple-element.16.count_message, f32[64,512]{1,0:T(8,128)S(1)} %get-tuple-element.17.own, f32[64,128]{1,0:T(8,128)S(1)} %get-tuple-element.18.count_own), custom_call_target="tpu_custom_call" | custom-call | tf_op jit(solution)/shard_map/exchange/pallas_call | solution.py:499
  36.4 0.7 %copy.12 = f32[64,512]{1,0:T(8,128)} copy(f32[64,512]{1,0:T(8,128)S(1)} %exchange.1) | data formatting | bytes 262144
Async XLA Ops:
  0.0 12.3 %copy-start = (f32[31,512]{1,0:T(8,128)S(1)}, f32[31,512]{1,0:T(8,128)}, u32[]{:S(2)}) copy-start(f32[31,512]{1,0:T(8,128)} %taps.1) | copy-start | bytes 190468
  0.0 0.7 %copy-start.1 = (s32[2048]{0:T(1024)S(1)}, s32[2048]{0:T(1024)}, u32[]{:S(2)}) copy-start(s32[2048]{0:T(1024)} %param.12) | copy-start | bytes 24580
  0.7 0.7 %copy-start.2 = (s32[2048]{0:T(1024)S(1)}, s32[2048]{0:T(1024)}, u32[]{:S(2)}) copy-start(s32[2048]{0:T(1024)} %param.11) | copy-start | bytes 24580
  1.4 0.7 %copy-start.3 = (f32[1024]{0:T(1024)S(1)}, f32[1024]{0:T(1024)}, u32[]{:S(2)}) copy-start(f32[1024]{0:T(1024)} %param.13) | copy-start | bytes 12292
  2.1 10.2 %copy-start.4 = (f32[512]{0:T(512)S(1)}, f32[512]{0:T(512)}, u32[]{:S(2)}) copy-start(f32[512]{0:T(512)} %param.17) | copy-start | bytes 6148
  2.1 10.2 %copy-start.5 = (f32[512]{0:T(512)S(1)}, f32[512]{0:T(512)}, u32[]{:S(2)}) copy-start(f32[512]{0:T(512)} %param.18) | copy-start | bytes 6148
